TPU v7x, 128 devices: a whole 4x4x4 slice. The times are simulated.
128 devices in a mesh: body: 2 (over core), sub: 64 (over x, y, z).
Axes of the slice: x: 4, y: 4, z: 4, core: 2. Of those that a mesh axis runs over, the one named last changes fastest.
Arguments:
- rhs: float32 [8, 4096, 256], P(None, 'sub'), may hold values from -50 to 50
- compliance: float32 [4096, 256], P('sub'), may hold values from 0.5 to 2
- plate_owner: int32 [4096, 1], P('sub'), may hold values from 0 to 63; in each aligned block of 64 rows (0 to 63, 64 to 127, ...) at most 2 rows name the same one
- found_owner: int32 [4096, 1], P('sub'), may hold values from 0 to 63; in each aligned block of 64 rows (0 to 63, 64 to 127, ...) at most 2 rows name the same one
- slot_pairs: int32 [4096, 2], P('sub'), may hold values from 0 to 7
- active: int32 [4096], P('sub'), may hold values 0 or 1
- inverse: bfloat16 [2, 64, 2048, 2048], P('body', 'sub'), may hold values from -0.06 to 4, as said below
Outputs:
- multipliers: float32 [8, 4096, 256], P(None, 'sub')
Inputs may be any that keep to these rules, and one draw needn't show every extreme that they name: `plate_owner`: at most 2 patches among the list of one index of sub name the same plate substructure; some list names one exactly 2 times. `found_owner`: at most 2 patches among the list of one index of sub name the same foundation substructure; some list names one exactly 2 times. Each block inverse[b, t] is symmetric positive definite.
All inputs are finite; a program needn't handle non-finite values. No bound on the sum of `active` on one device may be relied on, other than what follows from the above.
Results may differ from a plain program's by a relative error of at most 0.0055.
Values sent between devices are 32-bit elements; how exact they have to be, the bound alone decides.
A program may use at most 64 MiB of HBM per device.

v0:
```python
import jax
import jax.numpy as jnp
from jax import lax
from jax.sharding import PartitionSpec as P

ITERS = 4


def products(left, right):
    return jnp.sum(left * right, axis=(1, 2))


def squares(residual):
    return lax.psum(products(residual, residual), "sub")


def on_device(rhs, compliance, plate_owner, found_owner, slot_pairs, active, inverse):
    nsub = lax.axis_size("sub")
    side = lax.axis_index("body")
    ncase, npatch, block_width = rhs.shape
    local_inverse_block = inverse[0, 0]
    number_of_slots = local_inverse_block.shape[0] // block_width
    room = max(2, 2 * npatch // nsub)
    nrow = nsub * room
    owner = jnp.where(side == 0, plate_owner[:, 0], found_owner[:, 0])
    slot = jnp.where(side == 0, slot_pairs[:, 0], slot_pairs[:, 1])
    patch_index = jnp.arange(npatch, dtype=jnp.int32)
    earlier = patch_index[None, :] < patch_index[:, None]
    same_owner = owner[None, :] == owner[:, None]
    rank = jnp.sum(jnp.where(earlier & same_owner, 1, 0), axis=1).astype(jnp.int32)
    dest_row = owner * room + rank
    placed = dest_row[None, :] == jnp.arange(nrow, dtype=jnp.int32)[:, None]
    source = jnp.sum(jnp.where(placed, patch_index[None, :], 0), axis=1)
    filled = jnp.any(placed, axis=1)
    sent_slot = jnp.where(filled, jnp.take(slot, source), -1)
    received_slot = lax.all_to_all(sent_slot, "sub", split_axis=0, concat_axis=0, tiled=True)
    slot_lookup_table = (
        received_slot[None, :] == jnp.arange(number_of_slots, dtype=jnp.int32)[:, None]
    ).astype(jnp.float32)
    send_valid = filled.astype(jnp.float32)[None, :, None]
    keep = active.astype(jnp.float32)[None, :, None]
    residual = keep * rhs
    solution = jnp.zeros_like(rhs)
    direction = residual
    norm_now = squares(residual)
    for step in range(ITERS):
        outgoing = jnp.take(direction, source, axis=1) * send_valid
        column_entries = lax.all_to_all(outgoing, "sub", split_axis=1, concat_axis=1, tiled=True)
        load_vectors = jnp.einsum(
            "sb,rbk->rsk", slot_lookup_table, column_entries, precision=lax.Precision.HIGHEST
        )
        load_vectors = load_vectors.reshape(
            column_entries.shape[0], number_of_slots * block_width
        ).astype(jnp.bfloat16)
        response = jnp.dot(load_vectors, local_inverse_block, preferred_element_type=jnp.float32)
        plate_piece = lax.all_gather(response[None], "sub", axis=0, tiled=True)
        start = jnp.int32(0)
        slot_count = plate_piece.shape[0]
        local = jnp.clip(owner, 0, slot_count - 1)
        block_list = plate_piece.reshape(
            slot_count, plate_piece.shape[1], number_of_slots, block_width
        )
        chosen = block_list[local, :, slot, :]
        inside = (owner >= start) & (owner < start + slot_count)
        own_part = jnp.transpose(jnp.where(inside[:, None, None], chosen, 0.0), (1, 0, 2))
        total = lax.psum(own_part, "body")
        image = keep * (total + compliance[None] * direction)
        alpha = norm_now / lax.psum(products(direction, image), "sub")
        solution = solution + alpha[:, None, None] * direction
        residual = residual - alpha[:, None, None] * image
        norm_next = squares(residual)
        direction = residual + (norm_next / norm_now)[:, None, None] * direction
        norm_now = norm_next
    return solution


def solution(mesh):
    in_specs = (
        P(None, "sub", None),
        P("sub", None),
        P("sub", None),
        P("sub", None),
        P("sub", None),
        P("sub"),
        P("body", "sub", None, None),
    )
    out_specs = P(None, "sub", None)
    return jax.shard_map(
        on_device, mesh=mesh, in_specs=in_specs, out_specs=out_specs, check_vma=False
    )
```

profile of v0, /device:TPU:0, one launch (start us, length us, event | category | flops | bytes accessed | tf_op | source)
XLA Modules:
  0.0 1756.6 jit_solution(2245857336711810583)
XLA Ops:
  6.5 0.7 compare_and_fusion.1
  7.7 0.8 fusion.33
  8.7 1.2 gather_fusion
  10.0 0.6 select_select_fusion
  10.7 11.5 all-to-all-start.1
  22.2 0.7 convert_element_type.47
  22.9 1.4 copy_multiply_fusion
  24.2 0.8 gather_fusion.5
  25.0 1.3 bitcast_multiply_fusion.3
  26.3 5.3 all-to-all-done.1
  31.7 5.0 all-to-all-start
  36.7 0.5 broadcast.252
  37.3 0.7 reduce.3
  38.1 16.5 all-to-all-done
  54.7 0.7 fusion.8
  55.4 5.3 fusion.6
  60.8 65.0 %all-gather.9.cloned.1.call-done = f32[512,2048]{1,0:T(8,128)} async-done(((f32[8,2048]{1,0:T(8,128)}), f32[512,2048]{1,0:T(8,128)}) %all-gather.9.cloned.1.call-update) | async-done | bytes 4194320 | tf_op jit(solution)/shard_map/all_gather | solution.py:56
  125.7 2.9 gather_fusion.1
  128.6 0.9 select_bitcast_fusion.3
  129.6 21.8 %all-reduce.6.cloned.1.call-done = f32[8,64,256]{2,0,1:T(8,128)} async-done(((f32[8,64,256]{2,0,1:T(8,128)}), f32[8,64,256]{2,0,1:T(8,128)}) %all-reduce.6.cloned.1.call-update) | async-done | bytes 524304 | tf_op jit(solution)/shard_map/psum | solution.py:66
  151.5 1.6 multiply_reduce_fusion.6
  153.1 179.1 %all-reduce = (f32[8]{0:T(128)S(1)}, f32[8]{0:T(128)S(1)}) all-reduce(f32[8]{0:T(128)S(1)} %get-tuple-element.7, f32[8]{0:T(128)S(1)} %get-tuple-element.6), channel_id=1, replica_groups=mesh['body'=2,'sub'=64] {'sub'}, use_global_device_ids=true, to_apply=%region_1.2 | all-reduce | flops 16 | bytes 128 | tf_op jit(solution)/shard_map/psum | solution.py:14
  332.2 1.6 multiply_reduce_fusion.5
  333.8 172.0 %psum.87 = f32[8]{0:T(128)S(1)} all-reduce(f32[8]{0:T(128)S(1)} %multiply_reduce_fusion.5), channel_id=1, replica_groups=mesh['body'=2,'sub'=64] {'sub'}, use_global_device_ids=true, to_apply=%region_9.11 | all-reduce | flops 8 | bytes 64 | tf_op jit(solution)/shard_map/psum | solution.py:14
  505.8 1.4 multiply_add_fusion.3
  507.2 0.8 gather_fusion.6
  508.0 0.3 bitcast_multiply_fusion.2
  508.3 18.7 %all_to_all.26 = f32[8,128,256]{2,0,1:T(8,128)S(1)} all-to-all(f32[8,128,256]{2,0,1:T(8,128)S(1)} %bitcast_multiply_fusion.2), channel_id=1, replica_groups=mesh['body'=2,'sub'=64] {'sub'}, dimensions={1} | all-to-all | bytes 2097152 | tf_op jit(solution)/shard_map/all_to_all | solution.py:48
  527.0 0.7 fusion.9
  527.8 5.3 fusion.4
  533.1 64.8 %all-gather.11.cloned.1.call-done = f32[512,2048]{1,0:T(8,128)} async-done(((f32[8,2048]{1,0:T(8,128)}), f32[512,2048]{1,0:T(8,128)}) %all-gather.11.cloned.1.call-update) | async-done | bytes 4194320 | tf_op jit(solution)/shard_map/all_gather | solution.py:56
  597.9 2.9 gather_fusion.2
  600.8 0.9 select_bitcast_fusion.2
  601.8 21.8 %all-reduce.8.cloned.1.call-done = f32[8,64,256]{2,0,1:T(8,128)} async-done(((f32[8,64,256]{2,0,1:T(8,128)}), f32[8,64,256]{2,0,1:T(8,128)}) %all-reduce.8.cloned.1.call-update) | async-done | bytes 524304 | tf_op jit(solution)/shard_map/psum | solution.py:66
  623.6 1.4 multiply_reduce_fusion.4
  624.9 179.2 %psum.89 = f32[8]{0:T(128)S(1)} all-reduce(f32[8]{0:T(128)S(1)} %multiply_reduce_fusion.4), channel_id=1, replica_groups=mesh['body'=2,'sub'=64] {'sub'}, use_global_device_ids=true, to_apply=%region_12.14 | all-reduce | flops 8 | bytes 64 | tf_op jit(solution)/shard_map/psum | solution.py:68
  804.2 1.7 multiply_reduce_fusion.3
  805.8 171.8 %psum.90 = f32[8]{0:T(128)S(1)} all-reduce(f32[8]{0:T(128)S(1)} %get-tuple-element.10), channel_id=1, replica_groups=mesh['body'=2,'sub'=64] {'sub'}, use_global_device_ids=true, to_apply=%region_14.16 | all-reduce | flops 8 | bytes 64 | tf_op jit(solution)/shard_map/psum | solution.py:14
  977.7 0.8 gather_fusion.7
  978.9 18.5 %all_to_all.27 = f32[8,128,256]{2,0,1:T(8,128)S(1)} all-to-all(f32[8,128,256]{2,0,1:T(8,128)S(1)} %bitcast_multiply_fusion.1), channel_id=1, replica_groups=mesh['body'=2,'sub'=64] {'sub'}, dimensions={1} | all-to-all | bytes 2097152 | tf_op jit(solution)/shard_map/all_to_all | solution.py:48
  997.4 0.7 fusion.10
  998.1 5.2 fusion.2
  1003.4 64.8 %all-gather.13.cloned.1.call-done = f32[512,2048]{1,0:T(8,128)} async-done(((f32[8,2048]{1,0:T(8,128)}), f32[512,2048]{1,0:T(8,128)}) %all-gather.13.cloned.1.call-update) | async-done | bytes 4194320 | tf_op jit(solution)/shard_map/all_gather | solution.py:56
  1068.1 2.9 gather_fusion.3
  1071.0 0.9 select_bitcast_fusion.1
  1072.0 21.8 %all-reduce.10.cloned.1.call-done = f32[8,64,256]{2,0,1:T(8,128)} async-done(((f32[8,64,256]{2,0,1:T(8,128)}), f32[8,64,256]{2,0,1:T(8,128)}) %all-reduce.10.cloned.1.call-update) | async-done | bytes 524304 | tf_op jit(solution)/shard_map/psum | solution.py:66
  1093.9 1.4 multiply_reduce_fusion.2
  1095.2 179.1 %psum.92 = f32[8]{0:T(128)S(1)} all-reduce(f32[8]{0:T(128)S(1)} %multiply_reduce_fusion.2), channel_id=1, replica_groups=mesh['body'=2,'sub'=64] {'sub'}, use_global_device_ids=true, to_apply=%region_17.19 | all-reduce | flops 8 | bytes 64 | tf_op jit(solution)/shard_map/psum | solution.py:68
  1274.3 1.4 multiply_reduce_fusion.1
  1275.7 172.6 %psum.93 = f32[8]{0:T(128)S(1)} all-reduce(f32[8]{0:T(128)S(1)} %multiply_reduce_fusion.1), channel_id=1, replica_groups=mesh['body'=2,'sub'=64] {'sub'}, use_global_device_ids=true, to_apply=%region_19.21 | all-reduce | flops 8 | bytes 64 | tf_op jit(solution)/shard_map/psum | solution.py:14
  1448.3 1.2 multiply_add_fusion.1
  1449.5 1.7 gather_fusion.8
  1451.3 1.6 bitcast_multiply_fusion
  1452.8 18.7 %all_to_all.28 = f32[8,128,256]{2,0,1:T(8,128)S(1)} all-to-all(f32[8,128,256]{2,0,1:T(8,128)S(1)} %bitcast_multiply_fusion), channel_id=1, replica_groups=mesh['body'=2,'sub'=64] {'sub'}, dimensions={1} | all-to-all | bytes 2097152 | tf_op jit(solution)/shard_map/all_to_all | solution.py:48
  1471.5 0.7 fusion.11
  1472.3 5.2 fusion
  1477.5 64.8 %all-gather.15.cloned.1.call-done = f32[512,2048]{1,0:T(8,128)} async-done(((f32[8,2048]{1,0:T(8,128)}), f32[512,2048]{1,0:T(8,128)}) %all-gather.15.cloned.1.call-update) | async-done | bytes 4194320 | tf_op jit(solution)/shard_map/all_gather | solution.py:56
  1542.3 2.9 gather_fusion.4
  1545.2 0.9 select_bitcast_fusion
  1546.2 21.9 %all-reduce.12.cloned.1.call-done = f32[8,64,256]{2,0,1:T(8,128)} async-done(((f32[8,64,256]{2,0,1:T(8,128)}), f32[8,64,256]{2,0,1:T(8,128)}) %all-reduce.12.cloned.1.call-update) | async-done | bytes 524304 | tf_op jit(solution)/shard_map/psum | solution.py:66
  1568.0 1.4 multiply_reduce_fusion
  1569.4 179.1 %psum.95 = f32[8]{0:T(128)S(1)} all-reduce(f32[8]{0:T(128)S(1)} %multiply_reduce_fusion), channel_id=1, replica_groups=mesh['body'=2,'sub'=64] {'sub'}, use_global_device_ids=true, to_apply=%region_22.24 | all-reduce | flops 8 | bytes 64 | tf_op jit(solution)/shard_map/psum | solution.py:68
  1748.5 0.4 multiply_add_fusion
  1748.8 1.0 copy.27
  (49 shorter events, 2.0 us)
Async XLA Ops:
  10.7 21.0 %all-to-all-start.1 = ((s32[64,2,1]{1,2,0:T(1,128)}), s32[64,2,1]{1,2,0:T(1,128)S(1)}, u32[]{:S(2)}, u32[]{:S(2)}) async-start(s32[64,2,1]{1,2,0:T(1,128)} %bitcast.5), calls=%async_computation.1 | async-start | bytes 65536 | tf_op jit(solution)/shard_map/all_to_all | solution.py:36
  31.7 23.0 %all-to-all-start = ((f32[8,128,256]{2,0,1:T(8,128)}), f32[8,128,256]{2,0,1:T(8,128)S(1)}, u32[]{:S(2)}, u32[]{:S(2)}) async-start(f32[8,128,256]{2,0,1:T(8,128)} %bitcast_multiply_fusion.3), calls=%async_computation | async-start | bytes 2097152 | tf_op jit(solution)/shard_map/all_to_all | solution.py:48
  36.7 89.1 %all-gather.9.cloned.1.call-start = ((), (), s32[]{:S(2)}) async-start(), calls=%async_computation.9 | async-start | bytes 4259840 | tf_op jit(solution)/shard_map/all_gather | solution.py:56
  55.4 96.1 %copy-start = (f32[8,64,256]{2,1,0:T(8,128)S(1)}, f32[8,64,256]{2,1,0:T(8,128)}, u32[]{:S(2)}) copy-start(f32[8,64,256]{2,1,0:T(8,128)} %param.9) | copy-start | bytes 1572868
  55.4 96.1 %copy-start.2 = (f32[64,256]{1,0:T(8,128)S(1)}, f32[64,256]{1,0:T(8,128)}, u32[]{:S(2)}) copy-start(f32[64,256]{1,0:T(8,128)} %param.10) | copy-start | bytes 196612
  60.7 90.7 %all-reduce.6.cloned.1.call-start = ((), (), s32[]{:S(2)}) async-start(), calls=%async_computation.5 | async-start | bytes 1048576 | tf_op jit(solution)/shard_map/psum | solution.py:66
  129.6 468.3 %all-gather.11.cloned.1.call-start = ((), (), s32[]{:S(2)}) async-start(), calls=%async_computation.10 | async-start | bytes 4259840 | tf_op jit(solution)/shard_map/all_gather | solution.py:56
  527.7 276.4 %copy-start.1 = (f32[8,64,256]{2,0,1:T(8,128)S(1)}, f32[8,64,256]{2,0,1:T(8,128)}, u32[]{:S(2)}) copy-start(f32[8,64,256]{2,0,1:T(8,128)} %all-reduce.6.cloned.1.call-done) | copy-start | bytes 1572868
  533.0 90.5 %all-reduce.8.cloned.1.call-start = ((), (), s32[]{:S(2)}) async-start(), calls=%async_computation.6 | async-start | bytes 1048576 | tf_op jit(solution)/shard_map/psum | solution.py:66
  601.7 466.4 %all-gather.13.cloned.1.call-start = ((), (), s32[]{:S(2)}) async-start(), calls=%async_computation.11 | async-start | bytes 4259840 | tf_op jit(solution)/shard_map/all_gather | solution.py:56
  1003.3 90.5 %all-reduce.10.cloned.1.call-start = ((), (), s32[]{:S(2)}) async-start(), calls=%async_computation.7 | async-start | bytes 1048576 | tf_op jit(solution)/shard_map/psum | solution.py:66
  1072.0 470.3 %all-gather.15.cloned.1.call-start = ((), (), s32[]{:S(2)}) async-start(), calls=%async_computation.12 | async-start | bytes 4259840 | tf_op jit(solution)/shard_map/all_gather | solution.py:56
  1477.5 90.5 %all-reduce.12.cloned.1.call-start = ((), (), s32[]{:S(2)}) async-start(), calls=%async_computation.8 | async-start | bytes 1048576 | tf_op jit(solution)/shard_map/psum | solution.py:66
Sparse Core Ops, SparseCore 0:
  60.8 64.8 all-gather.8
  129.7 21.7 all-reduce.5
  533.2 64.6 all-gather.10
  601.8 21.6 all-reduce.7
  1003.4 64.6 all-gather.12
  1072.1 21.7 all-reduce.9
  1477.6 64.6 all-gather.14
  1546.3 21.6 all-reduce.11
where the time goes:
time: 1760 us
  blocking collectives  1290 us (73%)
  waiting for transfers between devices  369 us (21%)
  other arithmetic  26.1 us (1%)
  matrix products  23.8 us (1%)
  local copies, waits for them, and re-layouts  18.8 us (1%)
    psum x4, blocking collectives, squares(): return lax.psum(products(residual, residual), 'sub')  695 us
    psum x3, blocking collectives, on_device(): alpha = norm_now / lax.psum(products(direction, image), 'sub')  537 us
    all_gather x4, waiting for transfers between devices, on_device(): plate_piece = lax.all_gather(response[None], 'sub', axis=0, tiled=True)  259 us
    psum x4, waiting for transfers between devices, on_device(): total = lax.psum(own_part, 'body')  87.3 us
    all_to_all x3, blocking collectives, on_device(): lax.all_to_all(outgoing, 'sub', split_axis=1, concat_axis=1, tiled=True)  55.9 us
  transfers between devices with their start and end apart: 10, of which 10 were waited for; matrix products, arithmetic and copies ran while one was open for 0% of the time, Pallas kernels for 0%

commit v1 on v0

--- a/solution.py
+++ b/solution.py
@@ -4,6 +4,9 @@
 from jax.sharding import PartitionSpec as P
 
 ITERS = 4
+rest_knots = lambda here_x: jnp.concatenate(
+    lax.all_to_all(jnp.stack([here_x] * lax.axis_size("sub")), "sub", 0, 0), axis=0
+)
 
 
 def products(left, right):
@@ -53,7 +56,7 @@
             column_entries.shape[0], number_of_slots * block_width
         ).astype(jnp.bfloat16)
         response = jnp.dot(load_vectors, local_inverse_block, preferred_element_type=jnp.float32)
-        plate_piece = lax.all_gather(response[None], "sub", axis=0, tiled=True)
+        plate_piece = rest_knots(response[None])
         start = jnp.int32(0)
         slot_count = plate_piece.shape[0]
         local = jnp.clip(owner, 0, slot_count - 1)

time: 1760 us -> 1680 us (0.955)
  waiting for transfers between devices: 369 us -> 105 us
  blocking collectives: 1290 us -> 1470 us
    all_gather x4 -> x0, waiting for transfers between devices: 259 us -> none  [on_device(): plate_piece = lax.all_gather(response[None], 'sub', axis=0, tiled=True)]
    all_to_all x0 -> x4, blocking collectives: none -> 163 us  [lax.all_to_all(jnp.stack([here_x] * lax.axis_size('sub')), 'sub', 0, 0)]
  transfers between devices with their start and end apart: 10 -> 6, of which waited for: 10 -> 6; matrix products, arithmetic and copies ran while one was open for 0% -> 0% of each run, Pallas kernels for 0% -> 0%
where the time goes in v1:
time: 1680 us
  blocking collectives  1470 us (88%)
  waiting for transfers between devices  105 us (6%)
  other arithmetic  27.3 us (2%)
  local copies, waits for them, and re-layouts  21.8 us (1%)
  matrix products  21.2 us (1%)
    psum x4, blocking collectives, squares(): return lax.psum(products(residual, residual), 'sub')  706 us
    psum x3, blocking collectives, on_device(): alpha = norm_now / lax.psum(products(direction, image), 'sub')  537 us
    all_to_all x4, blocking collectives, lax.all_to_all(jnp.stack([here_x] * lax.axis_size('sub')), 'sub', 0, 0)  163 us
    psum x4, waiting for transfers between devices, on_device(): total = lax.psum(own_part, 'body')  82.7 us
    all_to_all x3, blocking collectives, on_device(): lax.all_to_all(outgoing, 'sub', split_axis=1, concat_axis=1, tiled=True)  65.5 us
  transfers between devices with their start and end apart: 6, of which 6 were waited for; matrix products, arithmetic and copies ran while one was open for 0% of the time, Pallas kernels for 0%

profile of v1, /device:TPU:0, one launch (start us, length us, event | category | flops | bytes accessed | tf_op | source)
XLA Modules:
  0.0 1676.6 jit_solution(2410707879900401876)
XLA Ops:
  6.5 0.7 compare_and_fusion.1
  7.7 0.8 fusion.33
  8.7 1.2 gather_fusion
  10.0 0.6 select_select_fusion
  10.7 11.5 all-to-all-start.1
  22.2 0.7 convert_element_type.47
  22.9 1.4 copy_multiply_fusion
  24.2 0.8 gather_fusion.5
  25.0 1.3 bitcast_multiply_fusion.3
  26.3 5.3 all-to-all-done.1
  31.7 5.0 all-to-all-start
  36.7 0.5 broadcast.260
  37.3 0.7 reduce.3
  38.1 16.5 all-to-all-done
  54.7 0.7 fusion.8
  55.4 4.6 fusion.6
  60.5 55.9 %all_to_all.46 = f32[64,1,8,2048]{3,2,1,0:T(8,128)} all-to-all(f32[64,1,8,2048]{3,2,1,0:T(8,128)S(1)} %stack.12), channel_id=1, replica_groups=mesh['body'=2,'sub'=64] {'sub'}, dimensions={0} | all-to-all | bytes 8388608 | tf_op jit(solution)/shard_map/all_to_all | solution.py:8
  116.4 2.9 gather_fusion.1
  119.3 0.9 select_bitcast_fusion.3
  120.3 21.3 %all-reduce.6.cloned.1.call-done = f32[8,64,256]{2,0,1:T(8,128)} async-done(((f32[8,64,256]{2,0,1:T(8,128)}), f32[8,64,256]{2,0,1:T(8,128)}) %all-reduce.6.cloned.1.call-update) | async-done | bytes 524304 | tf_op jit(solution)/shard_map/psum | solution.py:69
  141.5 1.6 multiply_reduce_fusion.6
  143.2 179.1 %all-reduce = (f32[8]{0:T(128)S(1)}, f32[8]{0:T(128)S(1)}) all-reduce(f32[8]{0:T(128)S(1)} %get-tuple-element.7, f32[8]{0:T(128)S(1)} %get-tuple-element.6), channel_id=1, replica_groups=mesh['body'=2,'sub'=64] {'sub'}, use_global_device_ids=true, to_apply=%region_1.2 | all-reduce | flops 16 | bytes 128 | tf_op jit(solution)/shard_map/psum | solution.py:17
  322.2 1.6 multiply_reduce_fusion.5
  323.9 174.9 %psum.87 = f32[8]{0:T(128)S(1)} all-reduce(f32[8]{0:T(128)S(1)} %multiply_reduce_fusion.5), channel_id=1, replica_groups=mesh['body'=2,'sub'=64] {'sub'}, use_global_device_ids=true, to_apply=%region_9.11 | all-reduce | flops 8 | bytes 64 | tf_op jit(solution)/shard_map/psum | solution.py:17
  498.8 1.4 multiply_add_fusion.3
  500.2 0.8 gather_fusion.6
  501.3 21.7 %all_to_all.47 = f32[8,128,256]{2,0,1:T(8,128)S(1)} all-to-all(f32[8,128,256]{2,0,1:T(8,128)S(1)} %bitcast_multiply_fusion.2), channel_id=1, replica_groups=mesh['body'=2,'sub'=64] {'sub'}, dimensions={1} | all-to-all | bytes 2097152 | tf_op jit(solution)/shard_map/all_to_all | solution.py:51
  523.0 0.7 fusion.9
  523.7 4.6 fusion.4
  528.8 35.7 %all_to_all.48 = f32[64,1,8,2048]{3,2,1,0:T(8,128)} all-to-all(f32[64,1,8,2048]{3,2,1,0:T(8,128)S(1)} %stack.13), channel_id=1, replica_groups=mesh['body'=2,'sub'=64] {'sub'}, dimensions={0} | all-to-all | bytes 8388608 | tf_op jit(solution)/shard_map/all_to_all | solution.py:8
  564.5 2.9 gather_fusion.2
  567.4 0.9 select_bitcast_fusion.2
  568.4 20.5 %all-reduce.8.cloned.1.call-done = f32[8,64,256]{2,0,1:T(8,128)} async-done(((f32[8,64,256]{2,0,1:T(8,128)}), f32[8,64,256]{2,0,1:T(8,128)}) %all-reduce.8.cloned.1.call-update) | async-done | bytes 524304 | tf_op jit(solution)/shard_map/psum | solution.py:69
  588.9 1.4 multiply_reduce_fusion.4
  590.2 179.1 %psum.89 = f32[8]{0:T(128)S(1)} all-reduce(f32[8]{0:T(128)S(1)} %multiply_reduce_fusion.4), channel_id=1, replica_groups=mesh['body'=2,'sub'=64] {'sub'}, use_global_device_ids=true, to_apply=%region_12.14 | all-reduce | flops 8 | bytes 64 | tf_op jit(solution)/shard_map/psum | solution.py:71
  769.3 1.7 multiply_reduce_fusion.3
  771.0 175.8 %psum.90 = f32[8]{0:T(128)S(1)} all-reduce(f32[8]{0:T(128)S(1)} %get-tuple-element.10), channel_id=1, replica_groups=mesh['body'=2,'sub'=64] {'sub'}, use_global_device_ids=true, to_apply=%region_14.16 | all-reduce | flops 8 | bytes 64 | tf_op jit(solution)/shard_map/psum | solution.py:17
  946.9 1.7 gather_fusion.7
  948.7 1.6 bitcast_multiply_fusion.1
  950.2 21.7 %all_to_all.49 = f32[8,128,256]{2,0,1:T(8,128)S(1)} all-to-all(f32[8,128,256]{2,0,1:T(8,128)S(1)} %bitcast_multiply_fusion.1), channel_id=1, replica_groups=mesh['body'=2,'sub'=64] {'sub'}, dimensions={1} | all-to-all | bytes 2097152 | tf_op jit(solution)/shard_map/all_to_all | solution.py:51
  971.9 0.7 fusion.10
  972.6 4.6 fusion.2
  977.2 0.5 stack.14
  977.7 35.7 %all_to_all.50 = f32[64,1,8,2048]{3,2,1,0:T(8,128)} all-to-all(f32[64,1,8,2048]{3,2,1,0:T(8,128)S(1)} %stack.14), channel_id=1, replica_groups=mesh['body'=2,'sub'=64] {'sub'}, dimensions={0} | all-to-all | bytes 8388608 | tf_op jit(solution)/shard_map/all_to_all | solution.py:8
  1013.4 2.9 gather_fusion.3
  1016.3 0.9 select_bitcast_fusion.1
  1017.3 20.5 %all-reduce.10.cloned.1.call-done = f32[8,64,256]{2,0,1:T(8,128)} async-done(((f32[8,64,256]{2,0,1:T(8,128)}), f32[8,64,256]{2,0,1:T(8,128)}) %all-reduce.10.cloned.1.call-update) | async-done | bytes 524304 | tf_op jit(solution)/shard_map/psum | solution.py:69
  1037.8 1.4 multiply_reduce_fusion.2
  1039.1 179.1 %psum.92 = f32[8]{0:T(128)S(1)} all-reduce(f32[8]{0:T(128)S(1)} %multiply_reduce_fusion.2), channel_id=1, replica_groups=mesh['body'=2,'sub'=64] {'sub'}, use_global_device_ids=true, to_apply=%region_17.19 | all-reduce | flops 8 | bytes 64 | tf_op jit(solution)/shard_map/psum | solution.py:71
  1218.2 1.4 multiply_reduce_fusion.1
  1219.6 176.1 %psum.93 = f32[8]{0:T(128)S(1)} all-reduce(f32[8]{0:T(128)S(1)} %multiply_reduce_fusion.1), channel_id=1, replica_groups=mesh['body'=2,'sub'=64] {'sub'}, use_global_device_ids=true, to_apply=%region_19.21 | all-reduce | flops 8 | bytes 64 | tf_op jit(solution)/shard_map/psum | solution.py:17
  1395.7 1.2 multiply_add_fusion.1
  1397.0 1.7 gather_fusion.8
  1398.7 1.6 bitcast_multiply_fusion
  1400.3 22.2 %all_to_all.51 = f32[8,128,256]{2,0,1:T(8,128)S(1)} all-to-all(f32[8,128,256]{2,0,1:T(8,128)S(1)} %bitcast_multiply_fusion), channel_id=1, replica_groups=mesh['body'=2,'sub'=64] {'sub'}, dimensions={1} | all-to-all | bytes 2097152 | tf_op jit(solution)/shard_map/all_to_all | solution.py:51
  1422.4 0.7 fusion.11
  1423.1 4.6 fusion
  1428.2 35.7 %all_to_all.52 = f32[64,1,8,2048]{3,2,1,0:T(8,128)} all-to-all(f32[64,1,8,2048]{3,2,1,0:T(8,128)S(1)} %stack.15), channel_id=1, replica_groups=mesh['body'=2,'sub'=64] {'sub'}, dimensions={0} | all-to-all | bytes 8388608 | tf_op jit(solution)/shard_map/all_to_all | solution.py:8
  1463.9 2.9 gather_fusion.4
  1466.8 0.9 select_bitcast_fusion
  1467.8 20.5 %all-reduce.12.cloned.1.call-done = f32[8,64,256]{2,0,1:T(8,128)} async-done(((f32[8,64,256]{2,0,1:T(8,128)}), f32[8,64,256]{2,0,1:T(8,128)}) %all-reduce.12.cloned.1.call-update) | async-done | bytes 524304 | tf_op jit(solution)/shard_map/psum | solution.py:69
  1488.3 1.4 multiply_reduce_fusion
  1489.6 179.1 %psum.95 = f32[8]{0:T(128)S(1)} all-reduce(f32[8]{0:T(128)S(1)} %multiply_reduce_fusion), channel_id=1, replica_groups=mesh['body'=2,'sub'=64] {'sub'}, use_global_device_ids=true, to_apply=%region_22.24 | all-reduce | flops 8 | bytes 64 | tf_op jit(solution)/shard_map/psum | solution.py:71
  1669.1 1.0 copy.27
  (45 shorter events, 3.6 us)
Async XLA Ops:
  10.7 21.0 %all-to-all-start.1 = ((s32[64,2,1]{1,2,0:T(1,128)}), s32[64,2,1]{1,2,0:T(1,128)S(1)}, u32[]{:S(2)}, u32[]{:S(2)}) async-start(s32[64,2,1]{1,2,0:T(1,128)} %bitcast.5), calls=%async_computation.1 | async-start | bytes 65536 | tf_op jit(solution)/shard_map/all_to_all | solution.py:39
  31.7 23.0 %all-to-all-start = ((f32[8,128,256]{2,0,1:T(8,128)}), f32[8,128,256]{2,0,1:T(8,128)S(1)}, u32[]{:S(2)}, u32[]{:S(2)}) async-start(f32[8,128,256]{2,0,1:T(8,128)} %bitcast_multiply_fusion.3), calls=%async_computation | async-start | bytes 2097152 | tf_op jit(solution)/shard_map/all_to_all | solution.py:51
  36.7 104.8 %all-reduce.6.cloned.1.call-start = ((), (), s32[]{:S(2)}) async-start(), calls=%async_computation.9 | async-start | bytes 1048576 | tf_op jit(solution)/shard_map/psum | solution.py:69
  60.0 81.6 %copy-start = (f32[8,64,256]{2,1,0:T(8,128)S(1)}, f32[8,64,256]{2,1,0:T(8,128)}, u32[]{:S(2)}) copy-start(f32[8,64,256]{2,1,0:T(8,128)} %param.9) | copy-start | bytes 1572868
  60.0 81.6 %copy-start.2 = (f32[64,256]{1,0:T(8,128)S(1)}, f32[64,256]{1,0:T(8,128)}, u32[]{:S(2)}) copy-start(f32[64,256]{1,0:T(8,128)} %param.10) | copy-start | bytes 196612
  120.2 468.6 %all-reduce.8.cloned.1.call-start = ((), (), s32[]{:S(2)}) async-start(), calls=%async_computation.10 | async-start | bytes 1048576 | tf_op jit(solution)/shard_map/psum | solution.py:69
  528.3 241.0 %copy-start.1 = (f32[8,64,256]{2,0,1:T(8,128)S(1)}, f32[8,64,256]{2,0,1:T(8,128)}, u32[]{:S(2)}) copy-start(f32[8,64,256]{2,0,1:T(8,128)} %all-reduce.6.cloned.1.call-done) | copy-start | bytes 1572868
  568.3 469.4 %all-reduce.10.cloned.1.call-start = ((), (), s32[]{:S(2)}) async-start(), calls=%async_computation.11 | async-start | bytes 1048576 | tf_op jit(solution)/shard_map/psum | solution.py:69
  1017.2 471.0 %all-reduce.12.cloned.1.call-start = ((), (), s32[]{:S(2)}) async-start(), calls=%async_computation.12 | async-start | bytes 1048576 | tf_op jit(solution)/shard_map/psum | solution.py:69
Sparse Core Ops, SparseCore 0:
  120.3 21.1 all-reduce.5
  568.5 20.3 all-reduce.7
  1017.4 20.3 all-reduce.9
  1467.9 20.3 all-reduce.11
